TPU v7x, 32 devices: a whole 2x2x4 slice. The times are simulated.
32 devices in a mesh: member: 4 (over y, x), slab: 2 (over core), tile: 4 (over z).
Axes of the slice: x: 2, y: 2, z: 4, core: 2. Of those that a mesh axis runs over, the one named last changes fastest.
Arguments:
- prior: float32 [128, 32768], P('member', ('slab', 'tile')), may hold values from -6 to 6
- sensitivity: bfloat16 [64, 16, 64, 512], P(('slab', 'tile')), may hold values from -0.0625 to 0.0625
- pattern: int32 [64, 16], P(('slab', 'tile')), may hold values from -1 to 63, as said below
- ownership: int32 [64], replicated, may hold values from 0 to 63, each once
- observed: float32 [4096], P(('slab', 'tile')), may hold values from -8 to 8
- obs_noise: float32 [4096], P(('slab', 'tile')), may hold values from 0.3 to 3
- perturbation: float32 [128, 4096], P('member', ('slab', 'tile')), may hold values from -5 to 5
Outputs:
- increment: float32 [128, 32768], P('member', ('slab', 'tile'))
- weights: float32 [128, 128], replicated
Inputs may be any that keep to these rules, and one draw needn't show every extreme that they name: In each row of pattern the first c entries are distinct observation block numbers and the remaining 16 - c entries are -1, with 4 <= c <= 16; some row is full and some row has exactly 4 live entries.
All inputs are finite; a program needn't handle non-finite values.
Results may differ from a plain program's by a relative error of at most 0.0042.
Values may be sent and summed in bfloat16 or wider, within the bound.
No kernel may reach another device: no remote copies, remote signals or barrier semaphores. Data moves between devices by JAX's collectives and lax.ppermute only.
A program may use at most 64 MiB of HBM per device.

v0:
```python
import math

import jax
import jax.numpy as jnp
from jax import lax
from jax.sharding import PartitionSpec as P


def local(prior, sensitivity, pattern, ownership, observed, obs_noise, perturbation):
    members_dev = prior.shape[0]
    members = members_dev * lax.axis_size("member")
    blocks_dev = sensitivity.shape[0]
    slot_count = sensitivity.shape[1]
    obs_block = sensitivity.shape[2]
    block_total = ownership.shape[0]
    obs_dev = observed.shape[0]
    owned_blocks = obs_dev // obs_block
    norm_scale = 1.0 / math.sqrt(members - 1)
    prior_bf = prior.astype(jnp.bfloat16)
    shaped = prior_bf.reshape(members_dev, blocks_dev, sensitivity.shape[3])
    contrib = jnp.einsum("bkop,mbp->bkmo", sensitivity, shaped, preferred_element_type=jnp.float32)
    contrib_rows = contrib.reshape(blocks_dev * slot_count, members_dev * obs_block)
    flat_pattern = pattern.reshape(blocks_dev * slot_count)
    storage_of = (
        jnp.zeros((block_total,), jnp.int32)
        .at[ownership]
        .set(jnp.arange(block_total, dtype=jnp.int32))
    )
    slot_rows = jnp.where(flat_pattern >= 0, storage_of[jnp.maximum(flat_pattern, 0)], block_total)
    row_count = owned_blocks * lax.axis_size(("slab", "tile"))
    target = jnp.where((slot_rows >= 0) & (slot_rows < row_count), slot_rows, row_count)
    placed = (
        jnp.zeros((row_count + 1, members_dev * obs_block), jnp.float32)
        .at[target]
        .add(contrib_rows)
    )
    owned_rows = lax.psum_scatter(
        placed[:row_count], ("slab", "tile"), scatter_dimension=0, tiled=True
    )
    predicted = (
        owned_rows.reshape(owned_blocks, members_dev, obs_block)
        .transpose(1, 0, 2)
        .reshape(members_dev, obs_dev)
    )
    mean_pred = lax.psum(jnp.sum(predicted, axis=0), "member") / members
    spread = (predicted - mean_pred) * norm_scale / obs_noise
    innovation = (observed - predicted) / obs_noise + perturbation
    spread_all, innov_all = (
        lax.all_gather(spread, "member", axis=0, tiled=True),
        lax.all_gather(innovation, "member", axis=0, tiled=True),
    )
    gram_local = jnp.einsum("mo,ko->mk", spread_all, spread_all, precision=lax.Precision.HIGHEST)
    cross_local = jnp.einsum("mo,ko->mk", spread_all, innov_all, precision=lax.Precision.HIGHEST)
    misfit_local = jnp.sum(innov_all * innov_all)
    gram_matrix, cross_term, misfit = lax.psum(
        (gram_local, cross_local, misfit_local), ("slab", "tile")
    )
    damping = misfit / (4.0 * members * members)
    system = gram_matrix + damping * jnp.eye(members, dtype=jnp.float32)
    factor = jnp.linalg.cholesky(system)
    weights = jax.scipy.linalg.cho_solve((factor, True), cross_term)
    centred = ((weights - jnp.mean(weights, axis=0, keepdims=True)) * norm_scale).astype(
        jnp.bfloat16
    )
    member_start = lax.axis_index("member") * members_dev
    own_cols = lax.dynamic_slice_in_dim(centred, member_start, members_dev, 1)
    increment = lax.dot_general(
        own_cols,
        lax.all_gather(prior_bf, "member", axis=0, tiled=True),
        (((0,), (0,)), ((), ())),
        preferred_element_type=jnp.float32,
    )
    return (increment, weights)


def solution(mesh):
    return jax.shard_map(
        local,
        mesh=mesh,
        in_specs=(
            P("member", ("slab", "tile")),
            P(("slab", "tile"), None, None, None),
            P(("slab", "tile"), None),
            P(),
            P(("slab", "tile")),
            P(("slab", "tile")),
            P("member", ("slab", "tile")),
        ),
        out_specs=(P("member", ("slab", "tile")), P()),
        check_vma=False,
    )
```

profile of v0, /device:TPU:0, one launch (start us, length us, event | category | flops | bytes accessed | tf_op | source)
XLA Modules:
  0.0 179.6 jit_solution(8055732935196030066)
XLA Ops:
  8.1 0.7 broadcast_maximum_fusion
  8.7 0.7 broadcast_compare_fusion
  9.4 1.1 convert_element_type.7
  10.6 7.4 %convolution_bitcast_fusion = f32[8,16,32,64]{3,2,1,0:T(8,128)S(1)} fusion(bf16[8,16,64,512]{3,2,1,0:T(8,128)(2,1)} %param.8, bf16[32,8,512,1]{2,1,0,3:T(8,128)(2,1)S(1)} %bitcast.39), kind=kOutput, calls=%fused_computation.3 | convolution fusion | flops 268435456 | bytes 9699328 | tf_op jit(solution)/shard_map/bkop,mbp->bkmo/dot_general | solution.py:21
  18.9 0.8 scatter_custom_fusion
  19.7 1.2 gather_fusion
  20.9 2.3 %scatter_custom_fusion.1 = f32[65,2048]{1,0:T(8,128)S(1)} fusion(s32[128]{0:T(128)S(1)} %fusion.15, f32[128,2048]{1,0:T(8,128)S(1)} %reshape.114, f32[]{:T(128)} %constant.70.clone.1), kind=kCustom, calls=%fused_computation.4 | custom fusion | flops 262144 | bytes 532484 | tf_op jit(solution)/shard_map/scatter-add | solution.py:35
  23.2 0.8 slice.24
  24.1 35.6 %reduce-scatter.2.cloned.1.call-done = f32[8,2048]{1,0:T(8,128)} async-done(((f32[64,2048]{1,0:T(8,128)}), f32[8,2048]{1,0:T(8,128)}) %reduce-scatter.2.cloned.1.call-update) | async-done | bytes 65552 | tf_op jit(solution)/shard_map/reduce_scatter | solution.py:37
  59.7 0.9 reshape.92
  61.0 9.8 %psum.28 = f32[512]{0:T(512)S(1)} all-reduce(f32[512]{0:T(512)S(1)} %reduce_sum.30), channel_id=1, replica_groups=mesh['member'=4,'slab'=2,'tile'=4] {'member'}, use_global_device_ids=true, to_apply=%region_4.5 | all-reduce | flops 512 | bytes 4096 | tf_op jit(solution)/shard_map/psum | solution.py:45
  70.8 8.4 %all_gather.10 = f32[128,512]{1,0:T(8,128)S(1)} all-gather(f32[32,512]{1,0:T(8,128)S(1)} %get-tuple-element.10), channel_id=1, replica_groups=mesh['member'=4,'slab'=2,'tile'=4] {'member'}, dimensions={0}, use_global_device_ids=true | all-gather | bytes 327680 | tf_op jit(solution)/shard_map/all_gather | solution.py:50
  79.2 8.6 %all_gather.9 = f32[128,512]{1,0:T(8,128)S(1)} all-gather(f32[32,512]{1,0:T(8,128)S(1)} %get-tuple-element.11), channel_id=1, replica_groups=mesh['member'=4,'slab'=2,'tile'=4] {'member'}, dimensions={0}, use_global_device_ids=true | all-gather | bytes 327680 | tf_op jit(solution)/shard_map/all_gather | solution.py:49
  87.8 1.0 fusion.21
  88.8 1.0 fusion.22
  91.1 14.5 %psum.30 = f32[]{:T(128)} all-reduce(f32[]{:T(128)} %multiply_reduce_fusion), channel_id=1, replica_groups=mesh['member'=4,'slab'=2,'tile'=4] {'slab','tile'}, use_global_device_ids=true, to_apply=%region_7.8 | all-reduce | flops 1 | bytes 8 | tf_op jit(solution)/shard_map/psum | solution.py:55
  106.3 36.6 %all-reduce.3.cloned.1.call-done = (f32[128,128]{1,0:T(8,128)}, f32[128,128]{1,0:T(8,128)}) async-done(((f32[128,128]{1,0:T(8,128)}, f32[128,128]{1,0:T(8,128)}), (f32[128,128]{1,0:T(8,128)}, f32[128,128]{1,0:T(8,128)})) %all-reduce.3.cloned.1.call-update) | async-done | bytes 131088 | tf_op jit(solution)/shard_map/psum | solution.py:55
  142.8 0.9 select_add_fusion
  143.8 0.9 fusion.8
  144.7 11.7 %cholesky.16 = f32[128,128]{1,0:T(8,128)S(1)} custom-call(f32[128,128]{1,0:T(8,128)S(1)} %fusion.8), custom_call_target="Cholesky" | custom-call | tf_op jit(solution)/shard_map/jit(cholesky)/cholesky | solution.py:60
  157.7 9.8 %custom-call.10 = f32[1,128,128]{1,2,0:T(8,128)S(1)} custom-call(f32[1,128,128]{2,1,0:T(8,128)S(1)} %fusion.3), custom_call_target="InvertDiagBlocksLowerTriangular" | custom-call | tf_op jit(solution)/shard_map/jit(_cho_solve)/triangular_solve | solution.py:61
  167.5 1.1 fusion.6
  169.0 0.7 copy.18
  169.9 2.3 %fusion.11 = f32[32,4096]{1,0:T(8,128)} fusion(bf16[128,4096]{1,0:T(8,128)(2,1)} %all-gather.2.cloned.1.call-done, f32[128,128]{0,1:T(8,128)S(1)} %get-tuple-element.13, s32[]{:T(128)S(6)} %select_n.47, f32[32]{0:T(128)S(1)} %dynamic-slice), kind=kOutput, calls=%fused_computation.25 | convolution fusion | flops 33566720 | bytes 1589764 | tf_op jit(solution)/shard_map/dot_general | solution.py:67
  (39 shorter events, 4.5 us)
Async XLA Ops:
  8.0 10.8 %copy-start.4 = (s32[64]{0:T(128)S(1)}, s32[64]{0:T(128)}, u32[]{:S(2)}) copy-start(s32[64]{0:T(128)} %param.10) | copy-start | bytes 772
  8.0 51.7 %reduce-scatter.2.cloned.1.call-start = ((), (), s32[]{:S(2)}) async-start(), calls=%async_computation.1 | async-start | bytes 589824 | tf_op jit(solution)/shard_map/reduce_scatter | solution.py:37
  10.5 13.6 %copy-start = (bf16[32,4096]{1,0:T(8,128)(2,1)}, bf16[32,4096]{1,0:T(8,128)(2,1)S(1)}, u32[]{:S(2)}) copy-start(bf16[32,4096]{1,0:T(8,128)(2,1)S(1)} %convert_element_type.7) | copy-start | bytes 786436
  10.6 60.2 %copy-start.1 = (f32[32,512]{1,0:T(8,128)S(1)}, f32[32,512]{1,0:T(8,128)}, u32[]{:S(2)}) copy-start(f32[32,512]{1,0:T(8,128)} %param.13) | copy-start | bytes 196612
  10.6 60.2 %copy-start.2 = (f32[512]{0:T(512)S(1)}, f32[512]{0:T(512)}, u32[]{:S(2)}) copy-start(f32[512]{0:T(512)} %param.11) | copy-start | bytes 6148
  10.6 60.2 %copy-start.3 = (f32[512]{0:T(512)S(1)}, f32[512]{0:T(512)}, u32[]{:S(2)}) copy-start(f32[512]{0:T(512)} %param.12) | copy-start | bytes 6148
  24.1 118.8 %all-reduce.3.cloned.1.call-start = ((), (), s32[]{:S(2)}) async-start(), calls=%async_computation.3 | async-start | bytes 262144 | tf_op jit(solution)/shard_map/psum | solution.py:55
  89.9 80.0 %all-gather.2.cloned.1.call-start = ((), (), s32[]{:S(2)}) async-start(), calls=%async_computation.2 | async-start | bytes 1310720 | tf_op jit(solution)/shard_map/all_gather | solution.py:69
Sparse Core Ops, SparseCore 0:
  24.2 35.5 reduce-scatter.1
  90.0 52.8 all-reduce.2
Sparse Core Ops, SparseCore 1:
  92.2 24.0 all-gather.1
where the time goes:
time: 180 us
  waiting for transfers between devices  72.7 us (40%)
  blocking collectives  41.3 us (23%)
  other arithmetic  30.1 us (17%)
  between operations  16.3 us (9%)
  matrix products  13.2 us (7%)
  local copies, waits for them, and re-layouts  5.85 us (3%)
    psum x1, waiting for transfers between devices, local(): lax.psum((gram_local, cross_local, misfit_local), ('slab', 'tile'))  36.6 us
    reduce_scatter x1, waiting for transfers between devices, local(): lax.psum_scatter(placed[:row_count], ('slab', 'tile'), scatter_dimension=...  35.6 us
    psum x1, blocking collectives, local(): lax.psum((gram_local, cross_local, misfit_local), ('slab', 'tile'))  14.5 us
    another operation x3, other arithmetic, local(): factor = jnp.linalg.cholesky(system)  12.4 us
    another operation x2, other arithmetic, local(): weights = jax.scipy.linalg.cho_solve((factor, True), cross_term)  10.5 us
    psum x1, blocking collectives, local(): mean_pred = lax.psum(jnp.sum(predicted, axis=0), 'member') / members  9.85 us
    all_gather x1, blocking collectives, local(): lax.all_gather(spread, 'member', axis=0, tiled=True)  8.57 us
    all_gather x1, blocking collectives, local(): lax.all_gather(innovation, 'member', axis=0, tiled=True)  8.39 us
  transfers between devices with their start and end apart: 3, of which 2 were waited for; matrix products, arithmetic and copies ran while one was open for 15% of the time, Pallas kernels for 0%

commit v1 on v0

v1 whole, which is shorter than its diff:
```python
import math

import jax
import jax.numpy as jnp
from jax import lax
from jax.sharding import PartitionSpec as P


def swap(x, axis, distance):
    size = lax.axis_size(axis)
    return lax.ppermute(x, axis, [(i, i ^ distance) for i in range(size)])


def digits(size):
    out, shift = [], 0
    while size > 1:
        radix = 4 if size % 4 == 0 else 2
        out.append((shift, radix))
        shift += radix.bit_length() - 1
        size //= radix
    return out[::-1]


def scatter_sum(chunks, axis):
    for shift, radix in digits(lax.axis_size(axis)):
        low = 1 << shift
        got = [
            [swap(chunks[d * low + r], axis, d << shift) for r in range(low)]
            for d in range(1, radix)
        ]
        chunks = [sum((g[r] for g in got), chunks[r]) for r in range(low)]
    return chunks[0]


def all_sum(x, axis):
    for shift, radix in digits(lax.axis_size(axis))[::-1]:
        x = sum((swap(x, axis, d << shift) for d in range(1, radix)), x)
    return x


def gather_xor(x, axis):
    return [x] + [swap(x, axis, r) for r in range(1, lax.axis_size(axis))]


def ordered(parts, index):
    stacked = jnp.stack(parts)
    return jnp.take(stacked, jnp.arange(len(parts)) ^ index, axis=0).reshape(
        len(parts) * parts[0].shape[0], *parts[0].shape[1:]
    )


def local(prior, sensitivity, pattern, ownership, observed, obs_noise, perturbation):
    members_dev = prior.shape[0]
    members = members_dev * lax.axis_size("member")
    blocks_dev, slot_count, obs_block, block_params = sensitivity.shape
    block_total = ownership.shape[0]
    obs_dev = observed.shape[0]
    owned_blocks = obs_dev // obs_block
    tiles = lax.axis_size("tile")
    norm_scale = 1.0 / math.sqrt(members - 1)
    member_at = lax.axis_index("member")
    slab_at = lax.axis_index("slab")
    tile_at = lax.axis_index("tile")
    prior_bf = prior.astype(jnp.bfloat16)

    shaped = prior_bf.reshape(members_dev, blocks_dev, block_params)
    contrib = jnp.einsum("bkop,mbp->bkmo", sensitivity, shaped, preferred_element_type=jnp.float32)
    contrib_rows = contrib.reshape(blocks_dev * slot_count, members_dev * obs_block)
    flat_pattern = pattern.reshape(blocks_dev * slot_count)
    storage_of = (
        jnp.zeros((block_total,), jnp.int32)
        .at[ownership]
        .set(jnp.arange(block_total, dtype=jnp.int32))
    )
    row = storage_of[jnp.maximum(flat_pattern, 0)]
    row = row ^ ((slab_at * tiles + tile_at) * owned_blocks)
    target = jnp.where(flat_pattern >= 0, row, block_total)
    placed = (
        jnp.zeros((block_total + 1, members_dev * obs_block), jnp.float32)
        .at[target]
        .add(contrib_rows)
    )
    half = tiles * owned_blocks
    chip = placed[:half] + swap(placed[half : 2 * half], "slab", 1)
    own = scatter_sum(
        [chip[r * owned_blocks : (r + 1) * owned_blocks] for r in range(tiles)], "tile"
    )
    predicted = (
        own.reshape(owned_blocks, members_dev, obs_block)
        .transpose(1, 0, 2)
        .reshape(members_dev, obs_dev)
    )
    noise_all = ordered(gather_xor(perturbation, "member"), member_at)
    predicted = ordered(gather_xor(predicted, "member"), member_at)
    mean_pred = jnp.mean(predicted, axis=0)
    spread = (predicted - mean_pred) * norm_scale / obs_noise
    innovation = (observed - predicted) / obs_noise + noise_all
    gram = jnp.einsum("mo,ko->mk", spread, spread, precision=lax.Precision.HIGHEST)
    cross = jnp.einsum("mo,ko->mk", spread, innovation, precision=lax.Precision.HIGHEST)
    misfit = jnp.sum(innovation * innovation)
    gram = gram + misfit / (4.0 * members * members) * jnp.eye(members, dtype=jnp.float32)
    both = jnp.concatenate([gram, cross], axis=1)
    rows = members // 2
    mine = lax.dynamic_slice_in_dim(both, slab_at * rows, rows, 0)
    other = lax.dynamic_slice_in_dim(both, (1 - slab_at) * rows, rows, 0)
    mine = all_sum(mine + swap(other, "slab", 1), "tile")
    both = ordered([mine, swap(mine, "slab", 1)], slab_at)
    system, cross = both[:, :members], both[:, members:]
    factor = jnp.linalg.cholesky(system)
    weights = jax.scipy.linalg.cho_solve((factor, True), cross)
    centred = ((weights - jnp.mean(weights, axis=0, keepdims=True)) * norm_scale).astype(
        jnp.bfloat16
    )
    own_cols = lax.dynamic_slice_in_dim(centred, member_at * members_dev, members_dev, 1)
    increment = lax.dot_general(
        own_cols,
        ordered(gather_xor(prior_bf, "member"), member_at),
        (((0,), (0,)), ((), ())),
        preferred_element_type=jnp.float32,
    )
    return (increment, weights)


def solution(mesh):
    return jax.shard_map(
        local,
        mesh=mesh,
        in_specs=(
            P("member", ("slab", "tile")),
            P(("slab", "tile"), None, None, None),
            P(("slab", "tile"), None),
            P(),
            P(("slab", "tile")),
            P(("slab", "tile")),
            P("member", ("slab", "tile")),
        ),
        out_specs=(P("member", ("slab", "tile")), P()),
        check_vma=False,
    )
```

time: 180 us -> 91.8 us (0.51)
  waiting for transfers between devices: 72.7 us -> 20.3 us
  blocking collectives: 41.3 us -> 0 us
  starting transfers between devices: 0.12 us -> 20.2 us
  between operations: 16.3 us -> 1.68 us
  matrix products: 13.2 us -> 9.88 us
  local copies, waits for them, and re-layouts: 5.85 us -> 7.91 us
    psum x1 -> x0, waiting for transfers between devices: 36.6 us -> none  [local(): lax.psum((gram_local, cross_local, misfit_local), ('slab', 'tile'))]
    reduce_scatter x1 -> x0, waiting for transfers between devices: 35.6 us -> none  [local(): lax.psum_scatter(placed[:row_count], ('slab', 'tile'), scatter_dimension=...]
    psum x2 -> x0, blocking collectives: 24.4 us -> none  [the longest x1 14.5 us: local(): lax.psum((gram_local, cross_local, misfit_local), ('slab', 'tile'))]
    ppermute x0 -> x18, waiting for transfers between devices: none -> 20.3 us  [swap(): return lax.ppermute(x, axis, [(i, i ^ distance) for i in range(size)])]
    ppermute x0 -> x18, starting transfers between devices: none -> 20.2 us  [swap(): return lax.ppermute(x, axis, [(i, i ^ distance) for i in range(size)])]
    all_gather x2 -> x0, blocking collectives: 17 us -> none  [the longest x1 8.57 us: local(): lax.all_gather(spread, 'member', axis=0, tiled=True)]
    dot_general x3, matrix products: 4.37 us -> 1.87 us  [the longest x1 1.12 us: local(): lax.dot_general(own_cols, ordered(gather_xor(prior_bf, 'member'), member_...]
    gather x1 -> x6, local copies, waits for them, and re-layouts: 1.23 us -> 3.62 us  [the longest x5 2.39 us: ordered(): jnp.take(stacked, jnp.arange(len(parts)) ^ index, axis=0)]
  transfers between devices with their start and end apart: 3 -> 18, of which waited for: 2 -> 8; matrix products, arithmetic and copies ran while one was open for 15% -> 25% of each run, Pallas kernels for 0% -> 0%
where the time goes in v1:
time: 91.8 us; the launch traced here: 91.5 us
  other arithmetic  31.5 us (34%)
  waiting for transfers between devices  20.3 us (22%)
  starting transfers between devices  20.2 us (22%)
  matrix products  9.88 us (11%)
  local copies, waits for them, and re-layouts  7.91 us (9%)
  between operations  1.68 us (2%)
    ppermute x18, waiting for transfers between devices, swap(): return lax.ppermute(x, axis, [(i, i ^ distance) for i in range(size)])  20.3 us
    ppermute x18, starting transfers between devices, swap(): return lax.ppermute(x, axis, [(i, i ^ distance) for i in range(size)])  20.2 us
    another operation x3, other arithmetic, local(): factor = jnp.linalg.cholesky(system)  12.4 us
    another operation x2, other arithmetic, local(): weights = jax.scipy.linalg.cho_solve((factor, True), cross)  10.5 us
    dot_general x1, matrix products, local(): jnp.einsum('bkop,mbp->bkmo', sensitivity, shaped, preferred_element_type=...  7.36 us
    scatter-add x1, other arithmetic, local(): placed = jnp.zeros((block_total + 1, members_dev * obs_block), jnp.float3...  3.16 us
    gather x5, local copies, waits for them, and re-layouts, ordered(): jnp.take(stacked, jnp.arange(len(parts)) ^ index, axis=0)  2.39 us
  transfers between devices with their start and end apart: 18, of which 8 were waited for; matrix products, arithmetic and copies ran while one was open for 25% of the time, Pallas kernels for 0%

profile of v1, /device:TPU:0, one launch (start us, length us, event | category | flops | bytes accessed | tf_op | source)
XLA Modules:
  0.0 91.5 jit_solution(10434898799313046143)
XLA Ops:
  0.6 3.0 %collective-permute-start.7 = (f32[32,512]{1,0:T(8,128)}, f32[32,512]{1,0:T(8,128)}, u32[]{:S(2)}, u32[]{:S(2)}) collective-permute-start(f32[32,512]{1,0:T(8,128)} %param.15), channel_id=1, source_target_pairs={{0,8},{8,0},{16,24},{24,16},{1,9},{9,1},{17,25},{25,17},{2,10},{10... | collective-permute-start | bytes 196616 | tf_op jit(solution)/shard_map/ppermute | solution.py:11
  3.7 1.5 %collective-permute-start.8 = (f32[32,512]{1,0:T(8,128)}, f32[32,512]{1,0:T(8,128)}, u32[]{:S(2)}, u32[]{:S(2)}) collective-permute-start(f32[32,512]{1,0:T(8,128)} %param.15), channel_id=1, source_target_pairs={{0,16},{8,24},{16,0},{24,8},{1,17},{9,25},{17,1},{25,9},{2,18},{10... | collective-permute-start | bytes 196616 | tf_op jit(solution)/shard_map/ppermute | solution.py:11
  7.4 1.1 %convert_element_type.7 = bf16[32,4096]{1,0:T(8,128)(2,1)S(1)} convert(f32[32,4096]{1,0:T(8,128)} %param.9) | non-fusion elementwise | flops 131072 | bytes 786432 | tf_op jit(solution)/shard_map/convert_element_type | solution.py:64
  8.7 7.4 %convolution_bitcast_fusion = f32[8,16,32,64]{3,2,1,0:T(8,128)S(1)} fusion(bf16[8,16,64,512]{3,2,1,0:T(8,128)(2,1)} %param.10, bf16[32,8,512,1]{2,1,0,3:T(8,128)(2,1)S(1)} %bitcast.62), kind=kOutput, calls=%fused_computation.7 | convolution fusion | flops 268435456 | bytes 9699328 | tf_op jit(solution)/shard_map/bkop,mbp->bkmo/dot_general | solution.py:67
  16.0 1.6 %reshape.244 = f32[128,2048]{1,0:T(8,128)} reshape(f32[8,16,32,64]{3,2,1,0:T(8,128)S(1)} %convolution_bitcast_fusion) | data formatting | bytes 2097152 | tf_op jit(solution)/shard_map/reshape | solution.py:68
  18.5 1.2 %gather_fusion = s32[128]{0:T(128)S(1)} fusion(s32[64]{0:T(128)S(1)} %scatter_custom_fusion, s32[1024]{0:T(1024)S(1)} %pad_clamp_fusion.3), kind=kCustom, calls=%fused_computation.2 | custom fusion | bytes 1536 | tf_op jit(solution)/shard_map/gather | solution.py:75
  19.7 3.2 %scatter_custom_fusion.1 = f32[65,2048]{1,0:T(8,128)S(1)} fusion(s32[128]{0:T(128)S(1)} %fusion.22, f32[128,2048]{1,0:T(8,128)} %reshape.244, f32[]{:T(128)} %constant.117.clone.1), kind=kCustom, calls=%fused_computation.11 | custom fusion | flops 262144 | bytes 532992 | tf_op jit(solution)/shard_map/scatter-add | solution.py:81
  23.1 1.4 %collective-permute-done = f32[32,2048]{1,0:T(8,128)S(1)} collective-permute-done((f32[32,2048]{1,0:T(8,128)S(1)}, f32[32,2048]{1,0:T(8,128)S(1)}, u32[]{:S(2)}, u32[]{:S(2)}) %collective-permute-start) | collective-permute-done | bytes 262176 | tf_op jit(solution)/shard_map/ppermute | solution.py:11
  24.6 1.6 %collective-permute-start.1 = (f32[8,2048]{1,0:T(8,128)S(1)}, f32[8,2048]{1,0:T(8,128)S(1)}, u32[]{:S(2)}, u32[]{:S(2)}) collective-permute-start(f32[8,2048]{1,0:T(8,128)S(1)} %get-tuple-element.12), channel_id=1, source_target_pairs={{0,1},{1,0},{2,3},{3,2},{4,5},{5,4},{6,7},{7,6},{8,9},{9,8},{10,11... | collective-permute-start | bytes 196616 | tf_op jit(solution)/shard_map/ppermute | solution.py:11
  26.2 2.6 %collective-permute-start.2 = (f32[8,2048]{1,0:T(8,128)S(1)}, f32[8,2048]{1,0:T(8,128)S(1)}, u32[]{:S(2)}, u32[]{:S(2)}) collective-permute-start(f32[8,2048]{1,0:T(8,128)S(1)} %get-tuple-element.14), channel_id=1, source_target_pairs={{0,2},{1,3},{2,0},{3,1},{4,6},{5,7},{6,4},{7,5},{8,10},{9,11},{10,... | collective-permute-start | bytes 196616 | tf_op jit(solution)/shard_map/ppermute | solution.py:11
  29.4 4.4 %collective-permute-done.2 = f32[8,2048]{1,0:T(8,128)S(1)} collective-permute-done((f32[8,2048]{1,0:T(8,128)S(1)}, f32[8,2048]{1,0:T(8,128)S(1)}, u32[]{:S(2)}, u32[]{:S(2)}) %collective-permute-start.2) | collective-permute-done | bytes 65568 | tf_op jit(solution)/shard_map/ppermute | solution.py:11
  36.6 1.5 %collective-permute-start.5 = (f32[32,512]{1,0:T(8,128)S(1)}, f32[32,512]{1,0:T(8,128)S(1)}, u32[]{:S(2)}, u32[]{:S(2)}) collective-permute-start(f32[32,512]{1,0:T(8,128)S(1)} %reshape.191), channel_id=1, source_target_pairs={{0,16},{8,24},{16,0},{24,8},{1,17},{9,25},{17,1},{25,9},{2,18},{10... | collective-permute-start | bytes 196616 | tf_op jit(solution)/shard_map/ppermute | solution.py:11
  38.2 1.2 %collective-permute-start.6 = (f32[32,512]{1,0:T(8,128)S(1)}, f32[32,512]{1,0:T(8,128)S(1)}, u32[]{:S(2)}, u32[]{:S(2)}) collective-permute-start(f32[32,512]{1,0:T(8,128)S(1)} %reshape.191), channel_id=1, source_target_pairs={{0,24},{8,16},{16,8},{24,0},{1,25},{9,17},{17,9},{25,1},{2,26},{10... | collective-permute-start | bytes 196616 | tf_op jit(solution)/shard_map/ppermute | solution.py:11
  41.5 1.6 %collective-permute-start.17 = (bf16[32,4096]{1,0:T(8,128)(2,1)S(1)}, bf16[32,4096]{1,0:T(8,128)(2,1)S(1)}, u32[]{:S(2)}, u32[]{:S(2)}) collective-permute-start(bf16[32,4096]{1,0:T(8,128)(2,1)S(1)} %convert_element_type.7), channel_id=1, source_target_pairs={{0,24},{8,16},{16,8},{24,0},{1,25},{9,17},{17,9},{25,1},{2,26},{10... | collective-permute-start | bytes 786440 | tf_op jit(solution)/shard_map/ppermute | solution.py:11
  43.1 6.9 %collective-permute-done.5 = f32[32,512]{1,0:T(8,128)S(1)} collective-permute-done((f32[32,512]{1,0:T(8,128)S(1)}, f32[32,512]{1,0:T(8,128)S(1)}, u32[]{:S(2)}, u32[]{:S(2)}) %collective-permute-start.5) | collective-permute-done | bytes 65568 | tf_op jit(solution)/shard_map/ppermute | solution.py:11
  53.4 0.9 collective-permute-done.10
  54.3 1.3 %collective-permute-start.11 = (f32[64,256]{1,0:T(8,128)S(1)}, f32[64,256]{1,0:T(8,128)S(1)}, u32[]{:S(2)}, u32[]{:S(2)}) collective-permute-start(f32[64,256]{1,0:T(8,128)S(1)} %fusion.6), channel_id=1, source_target_pairs={{0,1},{1,0},{2,3},{3,2},{4,5},{5,4},{6,7},{7,6},{8,9},{9,8},{10,11... | collective-permute-start | bytes 196616 | tf_op jit(solution)/shard_map/ppermute | solution.py:11
  55.6 0.9 %collective-permute-start.12 = (f32[64,256]{1,0:T(8,128)S(1)}, f32[64,256]{1,0:T(8,128)S(1)}, u32[]{:S(2)}, u32[]{:S(2)}) collective-permute-start(f32[64,256]{1,0:T(8,128)S(1)} %fusion.6), channel_id=1, source_target_pairs={{0,2},{1,3},{2,0},{3,1},{4,6},{5,7},{6,4},{7,5},{8,10},{9,11},{10,... | collective-permute-start | bytes 196616 | tf_op jit(solution)/shard_map/ppermute | solution.py:11
  56.5 2.2 %collective-permute-start.13 = (f32[64,256]{1,0:T(8,128)S(1)}, f32[64,256]{1,0:T(8,128)S(1)}, u32[]{:S(2)}, u32[]{:S(2)}) collective-permute-start(f32[64,256]{1,0:T(8,128)S(1)} %fusion.6), channel_id=1, source_target_pairs={{0,3},{1,2},{2,1},{3,0},{4,7},{5,6},{6,5},{7,4},{8,11},{9,10},{10,... | collective-permute-start | bytes 196616 | tf_op jit(solution)/shard_map/ppermute | solution.py:11
  59.5 4.3 %collective-permute-done.12 = f32[64,256]{1,0:T(8,128)S(1)} collective-permute-done((f32[64,256]{1,0:T(8,128)S(1)}, f32[64,256]{1,0:T(8,128)S(1)}, u32[]{:S(2)}, u32[]{:S(2)}) %collective-permute-start.12) | collective-permute-done | bytes 65568 | tf_op jit(solution)/shard_map/ppermute | solution.py:11
  64.1 1.0 %collective-permute-done.14 = f32[64,256]{1,0:T(8,128)S(1)} collective-permute-done((f32[64,256]{1,0:T(8,128)S(1)}, f32[64,256]{1,0:T(8,128)S(1)}, u32[]{:S(2)}, u32[]{:S(2)}) %collective-permute-start.14) | collective-permute-done | bytes 65568 | tf_op jit(solution)/shard_map/ppermute | solution.py:11
  66.0 11.7 %cholesky.16 = f32[128,128]{1,0:T(8,128)S(1)} custom-call(f32[128,128]{1,0:T(8,128)S(1)} %fusion.14), custom_call_target="Cholesky" | custom-call | tf_op jit(solution)/shard_map/jit(cholesky)/cholesky | solution.py:109
  79.1 9.8 %custom-call.10 = f32[1,128,128]{1,2,0:T(8,128)S(1)} custom-call(f32[1,128,128]{2,1,0:T(8,128)S(1)} %fusion.3), custom_call_target="InvertDiagBlocksLowerTriangular" | custom-call | tf_op jit(solution)/shard_map/jit(_cho_solve)/triangular_solve | solution.py:110
  90.3 1.1 %fusion.17 = f32[32,4096]{1,0:T(8,128)} fusion(bf16[128,4096]{1,0:T(8,128)(2,1)S(1)} %bitcast_select_fusion, f32[128,128]{0,1:T(8,128)S(1)} %get-tuple-element.16, s32[]{:T(128)S(6)} %select_n.95, f32[32]{0:T(128)S(1)} %dynamic-slice), kind=kOutput, calls=%fused_computation.49 | convolution fusion | flops 33566720 | bytes 1589764 | tf_op jit(solution)/shard_map/dot_general | solution.py:115
  (89 shorter events, 16.2 us)
Async XLA Ops:
  0.6 35.1 %collective-permute-start.7 = (f32[32,512]{1,0:T(8,128)}, f32[32,512]{1,0:T(8,128)}, u32[]{:S(2)}, u32[]{:S(2)}) collective-permute-start(f32[32,512]{1,0:T(8,128)} %param.15), channel_id=1, source_target_pairs={{0,8},{8,0},{16,24},{24,16},{1,9},{9,1},{17,25},{25,17},{2,10},{10... | collective-permute-start | bytes 196616 | tf_op jit(solution)/shard_map/ppermute | solution.py:11
  3.7 33.0 %collective-permute-start.8 = (f32[32,512]{1,0:T(8,128)}, f32[32,512]{1,0:T(8,128)}, u32[]{:S(2)}, u32[]{:S(2)}) collective-permute-start(f32[32,512]{1,0:T(8,128)} %param.15), channel_id=1, source_target_pairs={{0,16},{8,24},{16,0},{24,8},{1,17},{9,25},{17,1},{25,9},{2,18},{10... | collective-permute-start | bytes 196616 | tf_op jit(solution)/shard_map/ppermute | solution.py:11
  7.4 15.6 %copy-start = (f32[32,4096]{1,0:T(8,128)S(1)}, f32[32,4096]{1,0:T(8,128)}, u32[]{:S(2)}) copy-start(f32[32,4096]{1,0:T(8,128)} %param.9) | copy-start | bytes 1572868
  8.6 20.4 %copy-start.1 = (f32[32,512]{1,0:T(8,128)S(1)}, f32[32,512]{1,0:T(8,128)}, u32[]{:S(2)}) copy-start(f32[32,512]{1,0:T(8,128)} %param.15) | copy-start | bytes 196612
  8.6 42.1 %copy-start.2 = (f32[512]{0:T(512)S(1)}, f32[512]{0:T(512)}, u32[]{:S(2)}) copy-start(f32[512]{0:T(512)} %param.14) | copy-start | bytes 6148
  8.7 42.1 %copy-start.3 = (f32[512]{0:T(512)S(1)}, f32[512]{0:T(512)}, u32[]{:S(2)}) copy-start(f32[512]{0:T(512)} %param.13) | copy-start | bytes 6148
  22.9 1.6 %collective-permute-start = (f32[32,2048]{1,0:T(8,128)S(1)}, f32[32,2048]{1,0:T(8,128)S(1)}, u32[]{:S(2)}, u32[]{:S(2)}) collective-permute-start(f32[32,2048]{1,0:T(8,128)S(1)} %slice.59), channel_id=1, source_target_pairs={{0,4},{4,0},{1,5},{5,1},{2,6},{6,2},{3,7},{7,3},{8,12},{12,8},{9,1... | collective-permute-start | bytes 786440 | tf_op jit(solution)/shard_map/ppermute | solution.py:11
  24.6 4.5 %collective-permute-start.1 = (f32[8,2048]{1,0:T(8,128)S(1)}, f32[8,2048]{1,0:T(8,128)S(1)}, u32[]{:S(2)}, u32[]{:S(2)}) collective-permute-start(f32[8,2048]{1,0:T(8,128)S(1)} %get-tuple-element.12), channel_id=1, source_target_pairs={{0,1},{1,0},{2,3},{3,2},{4,5},{5,4},{6,7},{7,6},{8,9},{9,8},{10,11... | collective-permute-start | bytes 196616 | tf_op jit(solution)/shard_map/ppermute | solution.py:11
  26.2 7.5 %collective-permute-start.2 = (f32[8,2048]{1,0:T(8,128)S(1)}, f32[8,2048]{1,0:T(8,128)S(1)}, u32[]{:S(2)}, u32[]{:S(2)}) collective-permute-start(f32[8,2048]{1,0:T(8,128)S(1)} %get-tuple-element.14), channel_id=1, source_target_pairs={{0,2},{1,3},{2,0},{3,1},{4,6},{5,7},{6,4},{7,5},{8,10},{9,11},{10,... | collective-permute-start | bytes 196616 | tf_op jit(solution)/shard_map/ppermute | solution.py:11
  28.8 6.2 %collective-permute-start.3 = (f32[8,2048]{1,0:T(8,128)S(1)}, f32[8,2048]{1,0:T(8,128)S(1)}, u32[]{:S(2)}, u32[]{:S(2)}) collective-permute-start(f32[8,2048]{1,0:T(8,128)S(1)} %get-tuple-element.13), channel_id=1, source_target_pairs={{0,3},{1,2},{2,1},{3,0},{4,7},{5,6},{6,5},{7,4},{8,11},{9,10},{10,... | collective-permute-start | bytes 196616 | tf_op jit(solution)/shard_map/ppermute | solution.py:11
  29.0 9.1 %collective-permute-start.9 = (f32[32,512]{1,0:T(8,128)S(1)}, f32[32,512]{1,0:T(8,128)S(1)}, u32[]{:S(2)}, u32[]{:S(2)}) collective-permute-start(f32[32,512]{1,0:T(8,128)S(1)} %copy-done.1), channel_id=1, source_target_pairs={{0,24},{8,16},{16,8},{24,0},{1,25},{9,17},{17,9},{25,1},{2,26},{10... | collective-permute-start | bytes 196616 | tf_op jit(solution)/shard_map/ppermute | solution.py:11
  33.7 22.8 %collective-permute-start.15 = (bf16[32,4096]{1,0:T(8,128)(2,1)S(1)}, bf16[32,4096]{1,0:T(8,128)(2,1)S(1)}, u32[]{:S(2)}, u32[]{:S(2)}) collective-permute-start(bf16[32,4096]{1,0:T(8,128)(2,1)S(1)} %convert_element_type.7), channel_id=1, source_target_pairs={{0,8},{8,0},{16,24},{24,16},{1,9},{9,1},{17,25},{25,17},{2,10},{10... | collective-permute-start | bytes 786440 | tf_op jit(solution)/shard_map/ppermute | solution.py:11
  35.0 23.8 %collective-permute-start.16 = (bf16[32,4096]{1,0:T(8,128)(2,1)S(1)}, bf16[32,4096]{1,0:T(8,128)(2,1)S(1)}, u32[]{:S(2)}, u32[]{:S(2)}) collective-permute-start(bf16[32,4096]{1,0:T(8,128)(2,1)S(1)} %convert_element_type.7), channel_id=1, source_target_pairs={{0,16},{8,24},{16,0},{24,8},{1,17},{9,25},{17,1},{25,9},{2,18},{10... | collective-permute-start | bytes 786440 | tf_op jit(solution)/shard_map/ppermute | solution.py:11
  35.8 5.8 %collective-permute-start.4 = (f32[32,512]{1,0:T(8,128)S(1)}, f32[32,512]{1,0:T(8,128)S(1)}, u32[]{:S(2)}, u32[]{:S(2)}) collective-permute-start(f32[32,512]{1,0:T(8,128)S(1)} %reshape.191), channel_id=1, source_target_pairs={{0,8},{8,0},{16,24},{24,16},{1,9},{9,1},{17,25},{25,17},{2,10},{10... | collective-permute-start | bytes 196616 | tf_op jit(solution)/shard_map/ppermute | solution.py:11
  36.6 13.4 %collective-permute-start.5 = (f32[32,512]{1,0:T(8,128)S(1)}, f32[32,512]{1,0:T(8,128)S(1)}, u32[]{:S(2)}, u32[]{:S(2)}) collective-permute-start(f32[32,512]{1,0:T(8,128)S(1)} %reshape.191), channel_id=1, source_target_pairs={{0,16},{8,24},{16,0},{24,8},{1,17},{9,25},{17,1},{25,9},{2,18},{10... | collective-permute-start | bytes 196616 | tf_op jit(solution)/shard_map/ppermute | solution.py:11
  38.2 11.9 %collective-permute-start.6 = (f32[32,512]{1,0:T(8,128)S(1)}, f32[32,512]{1,0:T(8,128)S(1)}, u32[]{:S(2)}, u32[]{:S(2)}) collective-permute-start(f32[32,512]{1,0:T(8,128)S(1)} %reshape.191), channel_id=1, source_target_pairs={{0,24},{8,16},{16,8},{24,0},{1,25},{9,17},{17,9},{25,1},{2,26},{10... | collective-permute-start | bytes 196616 | tf_op jit(solution)/shard_map/ppermute | solution.py:11
  41.5 17.2 %collective-permute-start.17 = (bf16[32,4096]{1,0:T(8,128)(2,1)S(1)}, bf16[32,4096]{1,0:T(8,128)(2,1)S(1)}, u32[]{:S(2)}, u32[]{:S(2)}) collective-permute-start(bf16[32,4096]{1,0:T(8,128)(2,1)S(1)} %convert_element_type.7), channel_id=1, source_target_pairs={{0,24},{8,16},{16,8},{24,0},{1,25},{9,17},{17,9},{25,1},{2,26},{10... | collective-permute-start | bytes 786440 | tf_op jit(solution)/shard_map/ppermute | solution.py:11
  53.0 1.3 %collective-permute-start.10 = (f32[64,256]{1,0:T(8,128)S(1)}, f32[64,256]{1,0:T(8,128)S(1)}, u32[]{:S(2)}, u32[]{:S(2)}) collective-permute-start(f32[64,256]{1,0:T(8,128)S(1)} %fusion.4), channel_id=1, source_target_pairs={{0,4},{4,0},{1,5},{5,1},{2,6},{6,2},{3,7},{7,3},{8,12},{12,8},{9,1... | collective-permute-start | bytes 196616 | tf_op jit(solution)/shard_map/ppermute | solution.py:11
  54.3 5.2 %collective-permute-start.11 = (f32[64,256]{1,0:T(8,128)S(1)}, f32[64,256]{1,0:T(8,128)S(1)}, u32[]{:S(2)}, u32[]{:S(2)}) collective-permute-start(f32[64,256]{1,0:T(8,128)S(1)} %fusion.6), channel_id=1, source_target_pairs={{0,1},{1,0},{2,3},{3,2},{4,5},{5,4},{6,7},{7,6},{8,9},{9,8},{10,11... | collective-permute-start | bytes 196616 | tf_op jit(solution)/shard_map/ppermute | solution.py:11
  55.6 8.3 %collective-permute-start.12 = (f32[64,256]{1,0:T(8,128)S(1)}, f32[64,256]{1,0:T(8,128)S(1)}, u32[]{:S(2)}, u32[]{:S(2)}) collective-permute-start(f32[64,256]{1,0:T(8,128)S(1)} %fusion.6), channel_id=1, source_target_pairs={{0,2},{1,3},{2,0},{3,1},{4,6},{5,7},{6,4},{7,5},{8,10},{9,11},{10,... | collective-permute-start | bytes 196616 | tf_op jit(solution)/shard_map/ppermute | solution.py:11
  56.5 7.3 %collective-permute-start.13 = (f32[64,256]{1,0:T(8,128)S(1)}, f32[64,256]{1,0:T(8,128)S(1)}, u32[]{:S(2)}, u32[]{:S(2)}) collective-permute-start(f32[64,256]{1,0:T(8,128)S(1)} %fusion.6), channel_id=1, source_target_pairs={{0,3},{1,2},{2,1},{3,0},{4,7},{5,6},{6,5},{7,4},{8,11},{9,10},{10,... | collective-permute-start | bytes 196616 | tf_op jit(solution)/shard_map/ppermute | solution.py:11
  63.9 1.3 %collective-permute-start.14 = (f32[64,256]{1,0:T(8,128)S(1)}, f32[64,256]{1,0:T(8,128)S(1)}, u32[]{:S(2)}, u32[]{:S(2)}) collective-permute-start(f32[64,256]{1,0:T(8,128)S(1)} %add_add_fusion), channel_id=1, source_target_pairs={{0,4},{4,0},{1,5},{5,1},{2,6},{6,2},{3,7},{7,3},{8,12},{12,8},{9,1... | collective-permute-start | bytes 196616 | tf_op jit(solution)/shard_map/ppermute | solution.py:11

commit v2 on v0

v2 whole, which is shorter than its diff:
```python
import functools
import math

import jax
import jax.numpy as jnp
from jax import lax
from jax.experimental import pallas as pl
from jax.experimental.pallas import tpu as pltpu
from jax.sharding import PartitionSpec as P

EXACT = lax.Precision.HIGHEST
VMEM = pl.BlockSpec(memory_space=pltpu.VMEM)
SMEM = pl.BlockSpec(memory_space=pltpu.SMEM)
NT = (((1,), (1,)), ((), ()))


def swap(x, axis, distance):
    size = lax.axis_size(axis)
    return lax.ppermute(x, axis, [(i, i ^ distance) for i in range(size)])


def digits(size):
    out, shift = [], 0
    while size > 1:
        radix = 4 if size % 4 == 0 else 2
        out.append((shift, radix))
        shift += radix.bit_length() - 1
        size //= radix
    return out[::-1]


def gather_xor(x, axis):
    return [x] + [swap(x, axis, r) for r in range(1, lax.axis_size(axis))]


def contribute_kernel(
    owned, pattern_ref, ownership_ref, prior_ref, sens_ref, keep_ref, send_ref, bf_ref, acc, storage
):
    step = pl.program_id(0)
    tiles, members_dev, obs_dev = keep_ref.shape
    _, slots, obs_block, params = sens_ref.shape
    total = ownership_ref.shape[0]
    me = lax.axis_index("slab") * tiles + lax.axis_index("tile")

    @pl.when(step == 0)
    def _():
        def place(s, carry):
            storage[ownership_ref[s]] = s ^ (me * owned)
            return carry

        lax.fori_loop(0, total, place, 0, unroll=8)
        acc[...] = jnp.zeros_like(acc)

    rows = prior_ref[...].astype(jnp.bfloat16)
    bf_ref[...] = rows
    terms = lax.dot_general(
        rows, sens_ref[0].reshape(slots * obs_block, params), NT, preferred_element_type=jnp.float32
    )
    for k in range(slots):
        block = pattern_ref[step, k]
        at = jnp.where(block >= 0, storage[jnp.maximum(block, 0)], total)
        acc[at] += terms[:, k * obs_block : (k + 1) * obs_block]

    @pl.when(step == pl.num_programs(0) - 1)
    def _():
        group = max(1, 128 // obs_block)

        def flush(r, carry):
            for out, base in ((keep_ref, 0), (send_ref, tiles * owned)):
                for q in range(owned // group):
                    first = base + r * owned + q * group
                    out[r, :, q * group * obs_block : (q + 1) * group * obs_block] = (
                        jnp.concatenate([acc[first + g] for g in range(group)], axis=1)
                    )
            return carry

        lax.fori_loop(0, tiles, flush, 0)


def contribute(prior, sensitivity, pattern, ownership, obs_dev):
    members_dev = prior.shape[0]
    blocks, slots, obs_block, params = sensitivity.shape
    total = ownership.shape[0]
    tiles = lax.axis_size("tile")
    owned = obs_dev // obs_block
    half = jax.ShapeDtypeStruct((tiles, members_dev, obs_dev), jnp.float32)
    return pl.pallas_call(
        functools.partial(contribute_kernel, owned),
        grid_spec=pltpu.PrefetchScalarGridSpec(
            num_scalar_prefetch=2,
            grid=(blocks,),
            in_specs=[
                pl.BlockSpec((members_dev, params), lambda b, *_: (0, b)),
                pl.BlockSpec((1, slots, obs_block, params), lambda b, *_: (b, 0, 0, 0)),
            ],
            out_specs=[
                pl.BlockSpec(half.shape, lambda b, *_: (0, 0, 0)),
                pl.BlockSpec(half.shape, lambda b, *_: (0, 0, 0)),
                pl.BlockSpec((members_dev, params), lambda b, *_: (0, b)),
            ],
            scratch_shapes=[
                pltpu.VMEM((total + 1, members_dev, obs_block), jnp.float32),
                pltpu.SMEM((total,), jnp.int32),
            ],
        ),
        out_shape=[half, half, jax.ShapeDtypeStruct(prior.shape, jnp.bfloat16)],
        name="contribute",
    )(pattern, ownership, prior, sensitivity)


def gram_kernel(count, *refs):
    predicted, noise = refs[:count], refs[count : 2 * count]
    observed, sigma, keep, send, stack, whole = refs[2 * count :]
    members_dev = predicted[0].shape[0]
    members = members_dev * count
    at = lax.axis_index("member")
    for r in range(count):
        rows = pl.ds(pl.multiple_of((at ^ r) * members_dev, members_dev), members_dev)
        stack[rows, :] = predicted[r][...]
        whole_rows = pl.ds(pl.multiple_of(members + (at ^ r) * members_dev, members_dev), members_dev)
        stack[whole_rows, :] = noise[r][...]
    values = stack[:members, :]
    inverse = 1.0 / sigma[...]
    spread = (values - jnp.mean(values, axis=0, keepdims=True)) * (
        inverse * (1.0 / math.sqrt(members - 1))
    )
    innovation = (observed[...] - values) * inverse + stack[members:, :]
    stack[:members, :] = spread
    stack[members:, :] = innovation
    misfit = jnp.sum(jnp.sum(innovation * innovation, axis=0, keepdims=True), axis=1, keepdims=True)
    both = lax.dot_general(
        spread, stack[...], NT, precision=EXACT, preferred_element_type=jnp.float32
    )
    row = lax.broadcasted_iota(jnp.int32, both.shape, 0)
    col = lax.broadcasted_iota(jnp.int32, both.shape, 1)
    whole[...] = both + jnp.where(row == col, misfit * (1.0 / (4.0 * members * members)), 0.0)
    rows = members // 2
    side = lax.axis_index("slab")
    keep[...] = whole[pl.ds(pl.multiple_of(side * rows, rows), rows), :]
    send[...] = whole[pl.ds(pl.multiple_of((1 - side) * rows, rows), rows), :]


def gram(predicted, noise, observed, sigma):
    count = len(predicted)
    members_dev, obs_dev = predicted[0].shape
    members = members_dev * count
    half = jax.ShapeDtypeStruct((members // 2, 2 * members), jnp.float32)
    return pl.pallas_call(
        functools.partial(gram_kernel, count),
        in_specs=[VMEM] * (2 * count + 2),
        out_specs=[VMEM, VMEM],
        out_shape=[half, half],
        scratch_shapes=[
            pltpu.VMEM((2 * members, obs_dev), jnp.float32),
            pltpu.VMEM((members, 2 * members), jnp.float32),
        ],
        name="gram",
    )(*predicted, *noise, observed.reshape(1, obs_dev), sigma.reshape(1, obs_dev))


def update_kernel(count, *refs):
    mine, other = refs[:2]
    prior = refs[2 : 2 + count]
    increment, weights, both, cols, ensemble, sems = refs[2 + count :]
    members = weights.shape[0]
    members_dev = members // count
    at = lax.axis_index("member")
    side = lax.axis_index("slab")
    copies = []
    for r in range(count):
        rows = pl.ds(pl.multiple_of((at ^ r) * members_dev, members_dev), members_dev)
        copies.append(pltpu.make_async_copy(prior[r], ensemble.at[rows, :], sems.at[r]))
        copies[-1].start()
    half = members // 2
    both[pl.ds(pl.multiple_of(side * half, half), half), :] = mine[...]
    both[pl.ds(pl.multiple_of((1 - side) * half, half), half), :] = other[...]
    row = lax.broadcasted_iota(jnp.int32, (members, members), 0)
    col = lax.broadcasted_iota(jnp.int32, (members, members), 1)
    eye = jnp.where(row == col, 1.0, 0.0)
    system = both[:, :members]

    def total(x):
        return jnp.sum(jnp.sum(x, axis=0, keepdims=True), axis=1, keepdims=True)

    trace = total(system * eye)
    system = system + trace * (1.0 / (members * members))
    bound = jnp.max(jnp.sum(jnp.abs(system), axis=0, keepdims=True), axis=1, keepdims=True)
    scale = jnp.minimum(trace * (1.0 + 1.0 / members) / total(system * system), 1.9 / bound)
    power = eye - scale * system
    terms = both[:, members:] * scale

    def step(power, terms):
        pair = lax.dot_general(
            power,
            jnp.concatenate([power, terms], axis=1),
            (((1,), (0,)), ((), ())),
            precision=EXACT,
            preferred_element_type=jnp.float32,
        )
        return pair[:, :members], terms + pair[:, members:]

    for _ in range(5):
        power, terms = step(power, terms)

    def unfinished(carry):
        power, _, count = carry
        return (jnp.sum(power * power) > 1e-12) & (count < 40)

    def further(carry):
        power, terms, count = carry
        power, terms = step(power, terms)
        return power, terms, count + 1

    _, terms, _ = lax.while_loop(unfinished, further, (power, terms, 0))
    weights[...] = terms
    centred = (terms - jnp.mean(terms, axis=0, keepdims=True)) * (1.0 / math.sqrt(members - 1))
    cols[...] = centred.T
    own = cols[pl.ds(pl.multiple_of(at * members_dev, members_dev), members_dev), :].astype(
        jnp.bfloat16
    )
    for copy in copies:
        copy.wait()
    width = 512

    def multiply(n, carry):
        lanes = pl.ds(pl.multiple_of(n * width, width), width)
        increment[:, lanes] = jnp.dot(own, ensemble[:, lanes], preferred_element_type=jnp.float32)
        return carry

    lax.fori_loop(0, increment.shape[1] // width, multiply, 0, unroll=True)


def update(mine, other, prior):
    count = len(prior)
    members_dev, params = prior[0].shape
    members = members_dev * count
    return pl.pallas_call(
        functools.partial(update_kernel, count),
        in_specs=[VMEM, VMEM] + [pl.BlockSpec(memory_space=pl.ANY)] * count,
        out_specs=[VMEM, VMEM],
        out_shape=[
            jax.ShapeDtypeStruct((members_dev, params), jnp.float32),
            jax.ShapeDtypeStruct((members, members), jnp.float32),
        ],
        scratch_shapes=[
            pltpu.VMEM((members, 2 * members), jnp.float32),
            pltpu.VMEM((members, members), jnp.float32),
            pltpu.VMEM((members, params), jnp.bfloat16),
            pltpu.SemaphoreType.DMA((count,)),
        ],
        name="update",
    )(mine, other, *prior)


def local(prior, sensitivity, pattern, ownership, observed, obs_noise, perturbation):
    obs_dev = observed.shape[0]
    tiles = lax.axis_size("tile")
    keep, send, prior_bf = contribute(prior, sensitivity, pattern, ownership, obs_dev)
    got = swap(send, "slab", 1)
    chunks = [keep[r] + got[r] for r in range(tiles)]
    chunks, perturbation = lax.optimization_barrier((chunks, perturbation))
    noise = gather_xor(perturbation, "member")
    for shift, radix in digits(tiles):
        low = 1 << shift
        arrived = [
            [swap(chunks[d * low + r], "tile", d << shift) for r in range(low)]
            for d in range(1, radix)
        ]
        chunks = [sum((g[r] for g in arrived), chunks[r]) for r in range(low)]
    predicted = gather_xor(chunks[0], "member")
    keep, send = gram(predicted, noise, observed, obs_noise)
    keep, send, prior_bf = lax.optimization_barrier((keep, send, prior_bf))
    mine = keep + swap(send, "slab", 1)
    mine, prior_bf = lax.optimization_barrier((mine, prior_bf))
    ensemble = gather_xor(prior_bf, "member")
    for shift, radix in digits(tiles)[::-1]:
        mine = sum((swap(mine, "tile", d << shift) for d in range(1, radix)), mine)
    return tuple(update(mine, swap(mine, "slab", 1), ensemble))


def solution(mesh):
    return jax.shard_map(
        local,
        mesh=mesh,
        in_specs=(
            P("member", ("slab", "tile")),
            P(("slab", "tile"), None, None, None),
            P(("slab", "tile"), None),
            P(),
            P(("slab", "tile")),
            P(("slab", "tile")),
            P("member", ("slab", "tile")),
        ),
        out_specs=(P("member", ("slab", "tile")), P()),
        check_vma=False,
    )
```

time: 180 us -> 63.5 us (0.35)
  waiting for transfers between devices: 72.7 us -> 20.3 us
  blocking collectives: 41.3 us -> 0 us
  other arithmetic: 30.1 us -> 1.86 us
  starting transfers between devices: 0.12 us -> 20.8 us
  Pallas kernels: 0 us -> 17.3 us
  between operations: 16.3 us -> 0.73 us
  matrix products: 13.2 us -> 0 us
  local copies, waits for them, and re-layouts: 5.85 us -> 1.95 us
    psum x1 -> x0, waiting for transfers between devices: 36.6 us -> none  [local(): lax.psum((gram_local, cross_local, misfit_local), ('slab', 'tile'))]
    reduce_scatter x1 -> x0, waiting for transfers between devices: 35.6 us -> none  [local(): lax.psum_scatter(placed[:row_count], ('slab', 'tile'), scatter_dimension=...]
    psum x2 -> x0, blocking collectives: 24.4 us -> none  [the longest x1 14.5 us: local(): lax.psum((gram_local, cross_local, misfit_local), ('slab', 'tile'))]
    another operation x5 -> x0, other arithmetic: 22.9 us -> none  [the longest x3 12.4 us: local(): factor = jnp.linalg.cholesky(system)]
    ppermute x0 -> x18, starting transfers between devices: none -> 20.8 us  [swap(): return lax.ppermute(x, axis, [(i, i ^ distance) for i in range(size)])]
    ppermute x0 -> x18, waiting for transfers between devices: none -> 20.3 us  [swap(): return lax.ppermute(x, axis, [(i, i ^ distance) for i in range(size)])]
    pallas_call x0 -> x3, Pallas kernels: none -> 17.3 us  [the longest x1 10.1 us: contribute(): pl.pallas_call(functools.partial(contribute_kernel, owned), grid_spec=plt...]
    all_gather x2 -> x0, blocking collectives: 17 us -> none  [the longest x1 8.57 us: local(): lax.all_gather(spread, 'member', axis=0, tiled=True)]
  transfers between devices with their start and end apart: 3 -> 18, of which waited for: 2 -> 13; matrix products, arithmetic and copies ran while one was open for 15% -> 0% of each run, Pallas kernels for 0% -> 0%
where the time goes in v2:
time: 63.5 us; the launch traced here: 63 us
  starting transfers between devices  20.8 us (33%)
  waiting for transfers between devices  20.3 us (32%)
  Pallas kernels  17.3 us (27%)
  local copies, waits for them, and re-layouts  1.95 us (3%)
  other arithmetic  1.86 us (3%)
  between operations  0.73 us (1%)
    ppermute x18, starting transfers between devices, swap(): return lax.ppermute(x, axis, [(i, i ^ distance) for i in range(size)])  20.8 us
    ppermute x18, waiting for transfers between devices, swap(): return lax.ppermute(x, axis, [(i, i ^ distance) for i in range(size)])  20.3 us
    pallas_call x1, Pallas kernels, contribute(): pl.pallas_call(functools.partial(contribute_kernel, owned), grid_spec=plt...  10.1 us
    pallas_call x1, Pallas kernels, update(): pl.pallas_call(functools.partial(update_kernel, count), in_specs=[VMEM, V...  4.78 us
    pallas_call x1, Pallas kernels, gram(): pl.pallas_call(functools.partial(gram_kernel, count), in_specs=[VMEM] * (...  2.47 us
    unnamed x26, local copies, waits for them, and re-layouts  1.95 us
  transfers between devices with their start and end apart: 18, of which 13 were waited for; matrix products, arithmetic and copies ran while one was open for 0% of the time, Pallas kernels for 0%

profile of v2, /device:TPU:0, one launch (start us, length us, event | category | flops | bytes accessed | tf_op | source)
XLA Modules:
  0.0 63.0 jit_solution(15694931230979571944)
XLA Ops:
  0.6 10.1 %contribute.1 = (f32[4,32,512]{2,1,0:T(8,128)}, f32[4,32,512]{2,1,0:T(8,128)}, bf16[32,4096]{1,0:T(8,128)(2,1)}) custom-call(s32[8,16]{1,0:T(8,128)} %pattern_ref.1, s32[64]{0:T(128)} %ownership_ref.1, f32[32,4096]{1,0:T(8,128)} %prior_ref.1, bf16[8,16,64,512]{3,2,1,0:T(8,128)(2,1)} %sens_ref.1), custom_call_target="tpu_custom_call" | custom-call | tf_op jit(solution)/shard_map/contribute/pallas_call | solution.py:87
  11.2 1.4 %collective-permute-done = f32[4,32,512]{2,1,0:T(8,128)S(1)} collective-permute-done((f32[4,32,512]{2,1,0:T(8,128)}, f32[4,32,512]{2,1,0:T(8,128)S(1)}, u32[]{:S(2)}, u32[]{:S(2)}) %collective-permute-start) | collective-permute-done | bytes 262176 | tf_op jit(solution)/shard_map/ppermute | solution.py:19
  12.6 1.0 %fusion = (f32[32,512]{1,0:T(8,128)S(1)}, f32[32,512]{1,0:T(8,128)S(1)}, f32[32,512]{1,0:T(8,128)S(1)}, f32[32,512]{1,0:T(8,128)S(1)}) fusion(f32[4,32,512]{2,1,0:T(8,128)S(1)} %collective-permute-done, f32[4,32,512]{2,1,0:T(8,128)} %get-tuple-element.17), kind=kLoop, calls=%fused_computation.1 | loop fusion | flops 65536 | bytes 786432 | tf_op jit(solution)/shard_map/add | solution.py:260
  13.6 3.0 %collective-permute-start.1 = (f32[32,512]{1,0:T(8,128)S(1)}, f32[32,512]{1,0:T(8,128)S(1)}, u32[]{:S(2)}, u32[]{:S(2)}) collective-permute-start(f32[32,512]{1,0:T(8,128)S(1)} %get-tuple-element.20), channel_id=1, source_target_pairs={{0,1},{1,0},{2,3},{3,2},{4,5},{5,4},{6,7},{7,6},{8,9},{9,8},{10,11... | collective-permute-start | bytes 196616 | tf_op jit(solution)/shard_map/ppermute | solution.py:19
  16.6 2.6 %collective-permute-start.2 = (f32[32,512]{1,0:T(8,128)S(1)}, f32[32,512]{1,0:T(8,128)S(1)}, u32[]{:S(2)}, u32[]{:S(2)}) collective-permute-start(f32[32,512]{1,0:T(8,128)S(1)} %get-tuple-element.21), channel_id=1, source_target_pairs={{0,2},{1,3},{2,0},{3,1},{4,6},{5,7},{6,4},{7,5},{8,10},{9,11},{10,... | collective-permute-start | bytes 196616 | tf_op jit(solution)/shard_map/ppermute | solution.py:19
  19.2 2.6 %collective-permute-start.9 = (f32[32,512]{1,0:T(8,128)S(1)}, f32[32,512]{1,0:T(8,128)S(1)}, u32[]{:S(2)}, u32[]{:S(2)}) collective-permute-start(f32[32,512]{1,0:T(8,128)S(1)} %copy-done.6), channel_id=1, source_target_pairs={{0,24},{8,16},{16,8},{24,0},{1,25},{9,17},{17,9},{25,1},{2,26},{10... | collective-permute-start | bytes 196616 | tf_op jit(solution)/shard_map/ppermute | solution.py:19
  22.7 1.4 %collective-permute-done.2 = f32[32,512]{1,0:T(8,128)S(1)} collective-permute-done((f32[32,512]{1,0:T(8,128)S(1)}, f32[32,512]{1,0:T(8,128)S(1)}, u32[]{:S(2)}, u32[]{:S(2)}) %collective-permute-start.2) | collective-permute-done | bytes 65568 | tf_op jit(solution)/shard_map/ppermute | solution.py:19
  24.1 1.2 %collective-permute-done.3 = f32[32,512]{1,0:T(8,128)S(1)} collective-permute-done((f32[32,512]{1,0:T(8,128)S(1)}, f32[32,512]{1,0:T(8,128)S(1)}, u32[]{:S(2)}, u32[]{:S(2)}) %collective-permute-start.3) | collective-permute-done | bytes 65568 | tf_op jit(solution)/shard_map/ppermute | solution.py:19
  25.4 2.5 %collective-permute-start.6 = (f32[32,512]{1,0:T(8,128)S(1)}, f32[32,512]{1,0:T(8,128)S(1)}, u32[]{:S(2)}, u32[]{:S(2)}) collective-permute-start(f32[32,512]{1,0:T(8,128)S(1)} %add_add_fusion.1.refs_0_), channel_id=1, source_target_pairs={{0,24},{8,16},{16,8},{24,0},{1,25},{9,17},{17,9},{25,1},{2,26},{10... | collective-permute-start | bytes 196616 | tf_op jit(solution)/shard_map/ppermute | solution.py:19
  29.0 2.3 %collective-permute-done.6.refs_3_ = f32[32,512]{1,0:T(8,128)S(1)} collective-permute-done((f32[32,512]{1,0:T(8,128)S(1)}, f32[32,512]{1,0:T(8,128)S(1)}, u32[]{:S(2)}, u32[]{:S(2)}) %collective-permute-start.6) | collective-permute-done | bytes 65568 | tf_op jit(solution)/shard_map/ppermute | solution.py:19
  31.2 0.9 %collective-permute-done.5.refs_2_ = f32[32,512]{1,0:T(8,128)S(1)} collective-permute-done((f32[32,512]{1,0:T(8,128)S(1)}, f32[32,512]{1,0:T(8,128)S(1)}, u32[]{:S(2)}, u32[]{:S(2)}) %collective-permute-start.5) | collective-permute-done | bytes 65568 | tf_op jit(solution)/shard_map/ppermute | solution.py:19
  33.3 2.5 %gram.1 = (f32[64,256]{1,0:T(8,128)}, f32[64,256]{1,0:T(8,128)}) custom-call(f32[32,512]{1,0:T(8,128)} %copy-done.4, f32[32,512]{1,0:T(8,128)} %copy-done.12, f32[32,512]{1,0:T(8,128)} %copy-done.11, f32[32,512]{1,0:T(8,128)} %copy-done.10, f32[32,512]{1,0:T(8,128)} %refs_4_, f32[32,512]{1,0:T(8,128)} %copy-done.9, f32[32,512]{1,0:T(8,128)} %copy-done.8, ...), custom_call_target="tpu_custom_call" | custom-call | tf_op jit(solution)/shard_map/gram/pallas_call | solution.py:148
  35.8 1.5 %collective-permute-done.10 = f32[64,256]{1,0:T(8,128)S(1)} collective-permute-done((f32[64,256]{1,0:T(8,128)}, f32[64,256]{1,0:T(8,128)S(1)}, u32[]{:S(2)}, u32[]{:S(2)}) %collective-permute-start.10) | collective-permute-done | bytes 65568 | tf_op jit(solution)/shard_map/ppermute | solution.py:19
  37.2 0.9 %add.56 = f32[64,256]{1,0:T(8,128)S(1)} add(f32[64,256]{1,0:T(8,128)} %get-tuple-element.27, f32[64,256]{1,0:T(8,128)S(1)} %collective-permute-done.10) | non-fusion elementwise | flops 16384 | bytes 196608 | tf_op jit(solution)/shard_map/add | solution.py:273
  38.1 2.0 %collective-permute-start.13 = (f32[64,256]{1,0:T(8,128)S(1)}, f32[64,256]{1,0:T(8,128)S(1)}, u32[]{:S(2)}, u32[]{:S(2)}) collective-permute-start(f32[64,256]{1,0:T(8,128)S(1)} %add.56), channel_id=1, source_target_pairs={{0,3},{1,2},{2,1},{3,0},{4,7},{5,6},{6,5},{7,4},{8,11},{9,10},{10,... | collective-permute-start | bytes 196616 | tf_op jit(solution)/shard_map/ppermute | solution.py:19
  40.4 2.1 %collective-permute-start.11 = (f32[64,256]{1,0:T(8,128)S(1)}, f32[64,256]{1,0:T(8,128)S(1)}, u32[]{:S(2)}, u32[]{:S(2)}) collective-permute-start(f32[64,256]{1,0:T(8,128)S(1)} %add.56), channel_id=1, source_target_pairs={{0,1},{1,0},{2,3},{3,2},{4,5},{5,4},{6,7},{7,6},{8,9},{9,8},{10,11... | collective-permute-start | bytes 196616 | tf_op jit(solution)/shard_map/ppermute | solution.py:19
  42.6 1.5 %collective-permute-start.17 = (bf16[32,4096]{1,0:T(8,128)(2,1)}, bf16[32,4096]{1,0:T(8,128)(2,1)S(1)}, u32[]{:S(2)}, u32[]{:S(2)}) collective-permute-start(bf16[32,4096]{1,0:T(8,128)(2,1)} %get-tuple-element.31.refs_2_), channel_id=1, source_target_pairs={{0,24},{8,16},{16,8},{24,0},{1,25},{9,17},{17,9},{25,1},{2,26},{10... | collective-permute-start | bytes 786440 | tf_op jit(solution)/shard_map/ppermute | solution.py:19
  44.9 1.1 %collective-permute-start.15 = (bf16[32,4096]{1,0:T(8,128)(2,1)}, bf16[32,4096]{1,0:T(8,128)(2,1)S(1)}, u32[]{:S(2)}, u32[]{:S(2)}) collective-permute-start(bf16[32,4096]{1,0:T(8,128)(2,1)} %get-tuple-element.31.refs_2_), channel_id=1, source_target_pairs={{0,8},{8,0},{16,24},{24,16},{1,9},{9,1},{17,25},{25,17},{2,10},{10... | collective-permute-start | bytes 786440 | tf_op jit(solution)/shard_map/ppermute | solution.py:19
  46.0 0.9 %collective-permute-done.12 = f32[64,256]{1,0:T(8,128)S(1)} collective-permute-done((f32[64,256]{1,0:T(8,128)S(1)}, f32[64,256]{1,0:T(8,128)S(1)}, u32[]{:S(2)}, u32[]{:S(2)}) %collective-permute-start.12) | collective-permute-done | bytes 65568 | tf_op jit(solution)/shard_map/ppermute | solution.py:19
  47.0 1.2 %collective-permute-done.14.refs_1_ = f32[64,256]{1,0:T(8,128)S(1)} collective-permute-done((f32[64,256]{1,0:T(8,128)S(1)}, f32[64,256]{1,0:T(8,128)S(1)}, u32[]{:S(2)}, u32[]{:S(2)}) %collective-permute-start.14) | collective-permute-done | bytes 65568 | tf_op jit(solution)/shard_map/ppermute | solution.py:19
  48.3 4.6 %collective-permute-done.17.refs_5_ = bf16[32,4096]{1,0:T(8,128)(2,1)S(1)} collective-permute-done((bf16[32,4096]{1,0:T(8,128)(2,1)}, bf16[32,4096]{1,0:T(8,128)(2,1)S(1)}, u32[]{:S(2)}, u32[]{:S(2)}) %collective-permute-start.17) | collective-permute-done | bytes 262176 | tf_op jit(solution)/shard_map/ppermute | solution.py:19
  52.9 3.9 %collective-permute-done.16.refs_4_ = bf16[32,4096]{1,0:T(8,128)(2,1)S(1)} collective-permute-done((bf16[32,4096]{1,0:T(8,128)(2,1)}, bf16[32,4096]{1,0:T(8,128)(2,1)S(1)}, u32[]{:S(2)}, u32[]{:S(2)}) %collective-permute-start.16) | collective-permute-done | bytes 262176 | tf_op jit(solution)/shard_map/ppermute | solution.py:19
  57.5 0.7 %copy-done.3 = bf16[32,4096]{1,0:T(8,128)(2,1)} copy-done((bf16[32,4096]{1,0:T(8,128)(2,1)}, bf16[32,4096]{1,0:T(8,128)(2,1)S(1)}, u32[]{:S(2)}) %copy-start.3) | copy-done | bytes 262168
  58.2 4.8 %update.1 = (f32[32,4096]{1,0:T(8,128)}, f32[128,128]{1,0:T(8,128)}) custom-call(f32[64,256]{1,0:T(8,128)} %copy-done, f32[64,256]{1,0:T(8,128)} %copy-done.5, bf16[32,4096]{1,0:T(8,128)(2,1)} %get-tuple-element.31.refs_2_, bf16[32,4096]{1,0:T(8,128)(2,1)} %copy-done.3, bf16[32,4096]{1,0:T(8,128)(2,1)} %copy-done.2, bf16[32,4096]{1,0:T(8,128)(2,1)} %copy-done.1), custom_call_target="tpu_custom_call" | custom-call | tf_op jit(solution)/shard_map/update/pallas_call | solution.py:237
  (45 shorter events, 5.6 us)
Async XLA Ops:
  0.6 18.6 %copy-start.6 = (f32[32,512]{1,0:T(8,128)S(1)}, f32[32,512]{1,0:T(8,128)}, u32[]{:S(2)}) copy-start(f32[32,512]{1,0:T(8,128)} %refs_4_) | copy-start | bytes 196612
  10.7 1.9 %collective-permute-start = (f32[4,32,512]{2,1,0:T(8,128)}, f32[4,32,512]{2,1,0:T(8,128)S(1)}, u32[]{:S(2)}, u32[]{:S(2)}) collective-permute-start(f32[4,32,512]{2,1,0:T(8,128)} %get-tuple-element.18), channel_id=1, source_target_pairs={{0,4},{4,0},{1,5},{5,1},{2,6},{6,2},{3,7},{7,3},{8,12},{12,8},{9,1... | collective-permute-start | bytes 786440 | tf_op jit(solution)/shard_map/ppermute | solution.py:19
  13.6 8.7 %collective-permute-start.1 = (f32[32,512]{1,0:T(8,128)S(1)}, f32[32,512]{1,0:T(8,128)S(1)}, u32[]{:S(2)}, u32[]{:S(2)}) collective-permute-start(f32[32,512]{1,0:T(8,128)S(1)} %get-tuple-element.20), channel_id=1, source_target_pairs={{0,1},{1,0},{2,3},{3,2},{4,5},{5,4},{6,7},{7,6},{8,9},{9,8},{10,11... | collective-permute-start | bytes 196616 | tf_op jit(solution)/shard_map/ppermute | solution.py:19
  16.6 7.5 %collective-permute-start.2 = (f32[32,512]{1,0:T(8,128)S(1)}, f32[32,512]{1,0:T(8,128)S(1)}, u32[]{:S(2)}, u32[]{:S(2)}) collective-permute-start(f32[32,512]{1,0:T(8,128)S(1)} %get-tuple-element.21), channel_id=1, source_target_pairs={{0,2},{1,3},{2,0},{3,1},{4,6},{5,7},{6,4},{7,5},{8,10},{9,11},{10,... | collective-permute-start | bytes 196616 | tf_op jit(solution)/shard_map/ppermute | solution.py:19
  19.2 6.2 %collective-permute-start.3 = (f32[32,512]{1,0:T(8,128)S(1)}, f32[32,512]{1,0:T(8,128)S(1)}, u32[]{:S(2)}, u32[]{:S(2)}) collective-permute-start(f32[32,512]{1,0:T(8,128)S(1)} %get-tuple-element.22), channel_id=1, source_target_pairs={{0,3},{1,2},{2,1},{3,0},{4,7},{5,6},{6,5},{7,4},{8,11},{9,10},{10,... | collective-permute-start | bytes 196616 | tf_op jit(solution)/shard_map/ppermute | solution.py:19
  19.2 9.2 %collective-permute-start.9 = (f32[32,512]{1,0:T(8,128)S(1)}, f32[32,512]{1,0:T(8,128)S(1)}, u32[]{:S(2)}, u32[]{:S(2)}) collective-permute-start(f32[32,512]{1,0:T(8,128)S(1)} %copy-done.6), channel_id=1, source_target_pairs={{0,24},{8,16},{16,8},{24,0},{1,25},{9,17},{17,9},{25,1},{2,26},{10... | collective-permute-start | bytes 196616 | tf_op jit(solution)/shard_map/ppermute | solution.py:19
  21.8 7.1 %collective-permute-start.8 = (f32[32,512]{1,0:T(8,128)S(1)}, f32[32,512]{1,0:T(8,128)S(1)}, u32[]{:S(2)}, u32[]{:S(2)}) collective-permute-start(f32[32,512]{1,0:T(8,128)S(1)} %copy-done.6), channel_id=1, source_target_pairs={{0,16},{8,24},{16,0},{24,8},{1,17},{9,25},{17,1},{25,9},{2,18},{10... | collective-permute-start | bytes 196616 | tf_op jit(solution)/shard_map/ppermute | solution.py:19
  22.3 6.6 %collective-permute-start.7 = (f32[32,512]{1,0:T(8,128)S(1)}, f32[32,512]{1,0:T(8,128)S(1)}, u32[]{:S(2)}, u32[]{:S(2)}) collective-permute-start(f32[32,512]{1,0:T(8,128)S(1)} %copy-done.6), channel_id=1, source_target_pairs={{0,8},{8,0},{16,24},{24,16},{1,9},{9,1},{17,25},{25,17},{2,10},{10... | collective-permute-start | bytes 196616 | tf_op jit(solution)/shard_map/ppermute | solution.py:19
  25.4 7.3 %copy-start.4 = (f32[32,512]{1,0:T(8,128)}, f32[32,512]{1,0:T(8,128)S(1)}, u32[]{:S(2)}) copy-start(f32[32,512]{1,0:T(8,128)S(1)} %add_add_fusion.1.refs_0_) | copy-start | bytes 196612
  25.4 5.8 %collective-permute-start.6 = (f32[32,512]{1,0:T(8,128)S(1)}, f32[32,512]{1,0:T(8,128)S(1)}, u32[]{:S(2)}, u32[]{:S(2)}) collective-permute-start(f32[32,512]{1,0:T(8,128)S(1)} %add_add_fusion.1.refs_0_), channel_id=1, source_target_pairs={{0,24},{8,16},{16,8},{24,0},{1,25},{9,17},{17,9},{25,1},{2,26},{10... | collective-permute-start | bytes 196616 | tf_op jit(solution)/shard_map/ppermute | solution.py:19
  27.9 4.3 %collective-permute-start.5 = (f32[32,512]{1,0:T(8,128)S(1)}, f32[32,512]{1,0:T(8,128)S(1)}, u32[]{:S(2)}, u32[]{:S(2)}) collective-permute-start(f32[32,512]{1,0:T(8,128)S(1)} %add_add_fusion.1.refs_0_), channel_id=1, source_target_pairs={{0,16},{8,24},{16,0},{24,8},{1,17},{9,25},{17,1},{25,9},{2,18},{10... | collective-permute-start | bytes 196616 | tf_op jit(solution)/shard_map/ppermute | solution.py:19
  28.4 4.3 %copy-start.7 = (f32[32,512]{1,0:T(8,128)}, f32[32,512]{1,0:T(8,128)S(1)}, u32[]{:S(2)}) copy-start(f32[32,512]{1,0:T(8,128)S(1)} %collective-permute-done.9.refs_7_) | copy-start | bytes 196612
  28.4 4.3 %collective-permute-start.4 = (f32[32,512]{1,0:T(8,128)S(1)}, f32[32,512]{1,0:T(8,128)S(1)}, u32[]{:S(2)}, u32[]{:S(2)}) collective-permute-start(f32[32,512]{1,0:T(8,128)S(1)} %add_add_fusion.1.refs_0_), channel_id=1, source_target_pairs={{0,8},{8,0},{16,24},{24,16},{1,9},{9,1},{17,25},{25,17},{2,10},{10... | collective-permute-start | bytes 196616 | tf_op jit(solution)/shard_map/ppermute | solution.py:19
  35.8 1.5 %collective-permute-start.10 = (f32[64,256]{1,0:T(8,128)}, f32[64,256]{1,0:T(8,128)S(1)}, u32[]{:S(2)}, u32[]{:S(2)}) collective-permute-start(f32[64,256]{1,0:T(8,128)} %get-tuple-element.28), channel_id=1, source_target_pairs={{0,4},{4,0},{1,5},{5,1},{2,6},{6,2},{3,7},{7,3},{8,12},{12,8},{9,1... | collective-permute-start | bytes 196616 | tf_op jit(solution)/shard_map/ppermute | solution.py:19
  38.1 6.8 %collective-permute-start.13 = (f32[64,256]{1,0:T(8,128)S(1)}, f32[64,256]{1,0:T(8,128)S(1)}, u32[]{:S(2)}, u32[]{:S(2)}) collective-permute-start(f32[64,256]{1,0:T(8,128)S(1)} %add.56), channel_id=1, source_target_pairs={{0,3},{1,2},{2,1},{3,0},{4,7},{5,6},{6,5},{7,4},{8,11},{9,10},{10,... | collective-permute-start | bytes 196616 | tf_op jit(solution)/shard_map/ppermute | solution.py:19
  40.1 6.8 %collective-permute-start.12 = (f32[64,256]{1,0:T(8,128)S(1)}, f32[64,256]{1,0:T(8,128)S(1)}, u32[]{:S(2)}, u32[]{:S(2)}) collective-permute-start(f32[64,256]{1,0:T(8,128)S(1)} %add.56), channel_id=1, source_target_pairs={{0,2},{1,3},{2,0},{3,1},{4,6},{5,7},{6,4},{7,5},{8,10},{9,11},{10,... | collective-permute-start | bytes 196616 | tf_op jit(solution)/shard_map/ppermute | solution.py:19
  40.4 6.5 %collective-permute-start.11 = (f32[64,256]{1,0:T(8,128)S(1)}, f32[64,256]{1,0:T(8,128)S(1)}, u32[]{:S(2)}, u32[]{:S(2)}) collective-permute-start(f32[64,256]{1,0:T(8,128)S(1)} %add.56), channel_id=1, source_target_pairs={{0,1},{1,0},{2,3},{3,2},{4,5},{5,4},{6,7},{7,6},{8,9},{9,8},{10,11... | collective-permute-start | bytes 196616 | tf_op jit(solution)/shard_map/ppermute | solution.py:19
  42.6 10.3 %collective-permute-start.17 = (bf16[32,4096]{1,0:T(8,128)(2,1)}, bf16[32,4096]{1,0:T(8,128)(2,1)S(1)}, u32[]{:S(2)}, u32[]{:S(2)}) collective-permute-start(bf16[32,4096]{1,0:T(8,128)(2,1)} %get-tuple-element.31.refs_2_), channel_id=1, source_target_pairs={{0,24},{8,16},{16,8},{24,0},{1,25},{9,17},{17,9},{25,1},{2,26},{10... | collective-permute-start | bytes 786440 | tf_op jit(solution)/shard_map/ppermute | solution.py:19
  44.0 12.8 %collective-permute-start.16 = (bf16[32,4096]{1,0:T(8,128)(2,1)}, bf16[32,4096]{1,0:T(8,128)(2,1)S(1)}, u32[]{:S(2)}, u32[]{:S(2)}) collective-permute-start(bf16[32,4096]{1,0:T(8,128)(2,1)} %get-tuple-element.31.refs_2_), channel_id=1, source_target_pairs={{0,16},{8,24},{16,0},{24,8},{1,17},{9,25},{17,1},{25,9},{2,18},{10... | collective-permute-start | bytes 786440 | tf_op jit(solution)/shard_map/ppermute | solution.py:19
  44.9 12.0 %collective-permute-start.15 = (bf16[32,4096]{1,0:T(8,128)(2,1)}, bf16[32,4096]{1,0:T(8,128)(2,1)S(1)}, u32[]{:S(2)}, u32[]{:S(2)}) collective-permute-start(bf16[32,4096]{1,0:T(8,128)(2,1)} %get-tuple-element.31.refs_2_), channel_id=1, source_target_pairs={{0,8},{8,0},{16,24},{24,16},{1,9},{9,1},{17,25},{25,17},{2,10},{10... | collective-permute-start | bytes 786440 | tf_op jit(solution)/shard_map/ppermute | solution.py:19
  47.0 10.0 %copy-start = (f32[64,256]{1,0:T(8,128)}, f32[64,256]{1,0:T(8,128)S(1)}, u32[]{:S(2)}) copy-start(f32[64,256]{1,0:T(8,128)S(1)} %add_add_fusion.refs_0_) | copy-start | bytes 196612
  47.0 1.3 %collective-permute-start.14 = (f32[64,256]{1,0:T(8,128)S(1)}, f32[64,256]{1,0:T(8,128)S(1)}, u32[]{:S(2)}, u32[]{:S(2)}) collective-permute-start(f32[64,256]{1,0:T(8,128)S(1)} %add_add_fusion.refs_0_), channel_id=1, source_target_pairs={{0,4},{4,0},{1,5},{5,1},{2,6},{6,2},{3,7},{7,3},{8,12},{12,8},{9,1... | collective-permute-start | bytes 196616 | tf_op jit(solution)/shard_map/ppermute | solution.py:19
  48.3 8.6 %copy-start.5 = (f32[64,256]{1,0:T(8,128)}, f32[64,256]{1,0:T(8,128)S(1)}, u32[]{:S(2)}) copy-start(f32[64,256]{1,0:T(8,128)S(1)} %collective-permute-done.14.refs_1_) | copy-start | bytes 196612
  52.9 4.0 %copy-start.1 = (bf16[32,4096]{1,0:T(8,128)(2,1)}, bf16[32,4096]{1,0:T(8,128)(2,1)S(1)}, u32[]{:S(2)}) copy-start(bf16[32,4096]{1,0:T(8,128)(2,1)S(1)} %collective-permute-done.17.refs_5_) | copy-start | bytes 786436
  (7 other events, 11.6 us)
